TPU v7x, 256 devices: a whole 4x4x8 slice. The times are simulated.
256 devices in a mesh: tx: 4 (over y), ty: 2 (over z_lo), ea: 32 (over z_hi, x, core).
Axes of the slice: x: 4, y: 4, z: 8 (z_hi: 4, z_lo: 2; z = z_hi * 2 + z_lo), core: 2. Of those that a mesh axis runs over, the one named last changes fastest.
Arguments:
- science: float32 [32, 512, 512], P('ea', 'tx', 'ty'), may hold values from -6 to 6
- inv_variance: float32 [32, 512, 512], P('ea', 'tx', 'ty'), may hold values from 0.25 to 4
- psf_taps: float32 [32, 9], P('ea'), may hold values from 0.05 to 1
- epoch_times: int32 [32], replicated, may hold values from 0 to 256, as said below
- velocities: int32 [192, 2], P('ea'), may hold values from -15 to 15
Outputs:
- likelihood: float32 [192, 512, 512], P('ea', 'tx', 'ty')
Inputs may be any that keep to these rules, and one draw needn't show every extreme that they name: `epoch_times`: the first epoch has time 0 and the last has time 256.
All inputs are finite; a program needn't handle non-finite values.
Results may differ from a plain program's by a relative error of at most 0.0053.
Values may be sent and summed in bfloat16 or wider, within the bound.
A program may use at most 64 MiB of HBM per device.

v0:
```python
import jax
import jax.numpy as jnp
from jax import lax
from jax.sharding import PartitionSpec as P

REACH = 32
PR = 4


def extended(cells, sides, width):
    for axis, dim in sides:
        count = lax.axis_size(axis)
        ends = count - 1
        head = lax.slice_in_dim(cells, 0, width, axis=dim)
        tail = lax.slice_in_dim(cells, cells.shape[dim] - width, cells.shape[dim], axis=dim)
        cells = jnp.concatenate(
            [
                lax.ppermute(tail, axis, [(i, (i + 1) % count) for i in range(ends)]),
                cells,
                lax.ppermute(head, axis, [((i + 1) % count, i) for i in range(ends)]),
            ],
            axis=dim,
        )
    return cells


def blur(field, kern):
    count = kern.shape[1]
    rows = field.shape[1] - count + 1
    acc = kern[:, 0, None, None] * field[:, 0:rows, :]
    for k in range(1, count):
        acc = acc + kern[:, k, None, None] * field[:, k : k + rows, :]
    cols = acc.shape[2] - count + 1
    out = kern[:, 0, None, None] * acc[:, :, 0:cols]
    for k in range(1, count):
        out = out + kern[:, k, None, None] * acc[:, :, k : k + cols]
    return out


def spline_taps(speed, tvals):
    moved = jnp.floor_divide(speed * tvals, 8)
    whole = jnp.floor_divide(moved, 16)
    frac = (moved - 16 * whole).astype(jnp.float32) / 16.0
    frac2 = frac * frac
    frac3 = frac2 * frac
    weights = jnp.stack(
        [
            (1.0 - frac) ** 3 / 6.0,
            (3.0 * frac3 - 6.0 * frac2 + 4.0) / 6.0,
            (-3.0 * frac3 + 3.0 * frac2 + 3.0 * frac + 1.0) / 6.0,
            frac3 / 6.0,
        ],
        -1,
    )
    return (whole, weights.astype(jnp.bfloat16))


def band_matrix(whole, weights, count, span):
    target = lax.broadcasted_iota(jnp.int32, (1, count, span), 2)
    source = lax.broadcasted_iota(jnp.int32, (1, count, span), 1)
    offset = target - source - (REACH + whole - 1)[:, None, None]
    matrix = jnp.zeros((whole.shape[0], count, span), jnp.bfloat16)
    for a in range(4):
        matrix = matrix + jnp.where(
            offset == a, weights[:, a, None, None], jnp.zeros((), jnp.bfloat16)
        )
    return matrix


def stack_block(padded, tvals, velocities, out_rows, out_cols):
    pad_rows = padded.shape[2]
    pad_cols = padded.shape[3]

    def one_hyp(speed):
        whole_r, w_r = spline_taps(speed[0], tvals)
        whole_c, w_c = spline_taps(speed[1], tvals)
        row_band = band_matrix(whole_r, w_r, out_rows, pad_rows)
        col_band = band_matrix(whole_c, w_c, out_cols, pad_cols)
        moved_rows = jnp.einsum(
            "erp,eipk->eirk", row_band, padded, preferred_element_type=jnp.float32
        ).astype(jnp.bfloat16)
        return jnp.einsum("eirk,eck->irc", moved_rows, col_band, preferred_element_type=jnp.float32)

    return lax.map(one_hyp, velocities)


def shards(science, inv_variance, psf_taps, epoch_times, velocities):
    out_rows = science.shape[1]
    out_cols = science.shape[2]
    kern_p = psf_taps / jnp.sum(psf_taps, axis=1, keepdims=True)
    kern_q = kern_p * kern_p
    raw_pair = jnp.stack([science * inv_variance, inv_variance], 0)
    framed = extended(raw_pair, (("tx", 2), ("ty", 3)), PR)
    psi = blur(framed[0], kern_p).astype(jnp.bfloat16)
    phi = blur(framed[1], kern_q).astype(jnp.bfloat16)
    images = jnp.stack([psi, phi], 1)
    every_epoch = lax.all_gather(images, "ea", axis=0, tiled=True)
    padded = extended(every_epoch, (("tx", 2), ("ty", 3)), REACH)
    stacks = stack_block(padded, epoch_times, velocities, out_rows, out_cols)
    return stacks[:, 0] / jnp.sqrt(stacks[:, 1])


def solution(mesh):
    in_specs = (P("ea", "tx", "ty"), P("ea", "tx", "ty"), P("ea", None), P(), P("ea", None))
    out_specs = P("ea", "tx", "ty")
    return jax.shard_map(shards, mesh=mesh, in_specs=in_specs, out_specs=out_specs, check_vma=False)
```

profile of v0, /device:TPU:8, one launch (start us, length us, event | category | flops | bytes accessed | tf_op | source)
XLA Modules:
  0.0 320.8 jit_solution(10306133424879456887)
XLA Ops:
  8.2 3.5 %collective-permute-start = (f32[2,1,4,256]{3,2,1,0:T(4,128)S(1)}, f32[2,1,4,256]{3,2,1,0:T(4,128)S(1)}, u32[]{:S(2)}, u32[]{:S(2)}) collective-permute-start(f32[2,1,4,256]{3,2,1,0:T(4,128)S(1)} %get-tuple-element.184), channel_id=1, source_target_pairs={{0,64},{64,128},{128,192},{1,65},{65,129},{129,193},{2,66},{66,130... | collective-permute-start | bytes 24584 | tf_op jit(solution)/shard_map/ppermute | solution.py:18
  18.3 3.8 %collective-permute-start.2 = (f32[2,1,136,4]{3,2,1,0:T(8,128)S(1)}, f32[2,1,136,4]{3,2,1,0:T(8,128)S(1)}, u32[]{:S(2)}, u32[]{:S(2)}) collective-permute-start(f32[2,1,136,4]{3,2,1,0:T(8,128)S(1)} %get-tuple-element.182), channel_id=1, source_target_pairs={{0,32},{1,33},{2,34},{3,35},{4,36},{5,37},{6,38},{7,39},{8,40},{9,... | collective-permute-start | bytes 13064 | tf_op jit(solution)/shard_map/ppermute | solution.py:18
  24.7 4.4 %collective-permute-done.3 = f32[2,1,136,4]{3,2,1,0:T(8,128)S(1)} collective-permute-done((f32[2,1,136,4]{3,2,1,0:T(8,128)S(1)}, f32[2,1,136,4]{3,2,1,0:T(8,128)S(1)}, u32[]{:S(2)}, u32[]{:S(2)}) %collective-permute-start.3) | collective-permute-done | bytes 4384 | tf_op jit(solution)/shard_map/ppermute | solution.py:20
  30.3 6.0 %fusion.111 = f32[1,128,264]{2,1,0:T(8,128)S(1)} fusion(f32[1,136,264]{2,1,0:T(8,128)S(1)} %get-tuple-element.180, f32[]{:T(128)} %bitcast.29, f32[]{:T(128)} %bitcast.28, f32[]{:T(128)} %bitcast.27, f32[]{:T(128)} %bitcast.26, f32[]{:T(128)} %bitcast.25, f32[]{:T(128)} %bitcast.24, f32[]{:T(128)} %bitcast.23, f32[]{:T(128)} %bitcast.22, f32[]{:T(128)} %bitcast.18), kind=kLoop, calls=%fused_computation.141 | loop fusion | flops 574464 | bytes 1351716 | tf_op jit(solution)/shard_map/add | solution.py:32
  36.3 6.2 %fusion.137 = bf16[1,1,128,256]{3,2,1,0:T(8,128)(2,1)S(1)} fusion(f32[1,128,264]{2,1,0:T(8,128)S(1)} %fusion.111, f32[]{:T(128)} %bitcast.29, f32[]{:T(128)} %bitcast.28, f32[]{:T(128)} %bitcast.27, f32[]{:T(128)} %bitcast.26, f32[]{:T(128)} %bitcast.25, f32[]{:T(128)} %bitcast.24, f32[]{:T(128)} %bitcast.23, f32[]{:T(128)} %bitcast.22, f32[]{:T(128)} %bitcast.18), kind=kLoop, calls=%fused_computation.195 | loop fusion | flops 589824 | bytes 1245220 | tf_op jit(solution)/shard_map/stack | solution.py:96
  42.4 5.7 %fusion.103 = f32[1,128,264]{2,1,0:T(8,128)S(1)} fusion(f32[1,136,264]{2,1,0:T(8,128)S(1)} %get-tuple-element.181, f32[]{:T(128)} %bitcast.40, f32[]{:T(128)} %bitcast.39, f32[]{:T(128)} %bitcast.38, f32[]{:T(128)} %bitcast.37, f32[]{:T(128)} %bitcast.36, f32[]{:T(128)} %bitcast.35, f32[]{:T(128)} %bitcast.34, f32[]{:T(128)} %bitcast.33, f32[]{:T(128)} %bitcast.31), kind=kLoop, calls=%fused_computation.124 | loop fusion | flops 574464 | bytes 1351716 | tf_op jit(solution)/shard_map/add | solution.py:32
  48.2 5.9 %fusion.138 = bf16[1,1,128,256]{3,2,1,0:T(8,128)(2,1)S(1)} fusion(f32[1,128,264]{2,1,0:T(8,128)S(1)} %fusion.103, f32[]{:T(128)} %bitcast.40, f32[]{:T(128)} %bitcast.39, f32[]{:T(128)} %bitcast.38, f32[]{:T(128)} %bitcast.37, f32[]{:T(128)} %bitcast.36, f32[]{:T(128)} %bitcast.35, f32[]{:T(128)} %bitcast.34, f32[]{:T(128)} %bitcast.33, f32[]{:T(128)} %bitcast.31), kind=kLoop, calls=%fused_computation.196 | loop fusion | flops 589824 | bytes 1245220 | tf_op jit(solution)/shard_map/stack | solution.py:96
  54.7 62.2 %all-gather.2.cloned.1.call-done = bf16[32,2,128,256]{3,2,1,0:T(8,128)(2,1)} async-done(((bf16[1,2,128,256]{3,2,1,0:T(8,128)(2,1)}), bf16[32,2,128,256]{3,2,1,0:T(8,128)(2,1)}) %all-gather.2.cloned.1.call-update) | async-done | bytes 4194320 | tf_op jit(solution)/shard_map/all_gather | solution.py:97
  118.8 3.4 %collective-permute-start.4 = (bf16[32,2,32,256]{3,2,1,0:T(8,128)(2,1)S(1)}, bf16[32,2,32,256]{3,2,1,0:T(8,128)(2,1)S(1)}, u32[]{:S(2)}, u32[]{:S(2)}) collective-permute-start(bf16[32,2,32,256]{3,2,1,0:T(8,128)(2,1)S(1)} %get-tuple-element.179), channel_id=1, source_target_pairs={{0,64},{64,128},{128,192},{1,65},{65,129},{129,193},{2,66},{66,130... | collective-permute-start | bytes 3145736 | tf_op jit(solution)/shard_map/ppermute | solution.py:18
  124.7 21.3 %collective-permute-done.4 = bf16[32,2,32,256]{3,2,1,0:T(8,128)(2,1)S(1)} collective-permute-done((bf16[32,2,32,256]{3,2,1,0:T(8,128)(2,1)S(1)}, bf16[32,2,32,256]{3,2,1,0:T(8,128)(2,1)S(1)}, u32[]{:S(2)}, u32[]{:S(2)}) %collective-permute-start.4) | collective-permute-done | bytes 1048608 | tf_op jit(solution)/shard_map/ppermute | solution.py:18
  149.2 3.7 %fusion.141 = (bf16[32,2,192,32]{3,2,1,0:T(8,128)(2,1)}, bf16[32,2,192,32]{3,2,1,0:T(8,128)(2,1)S(1)}) fusion(bf16[32,2,192,256]{3,2,1,0:T(8,128)(2,1)S(1)} %constant_dynamic-update-slice_fusion), kind=kLoop, calls=%fused_computation.205 | loop fusion | bytes 3145728 | tf_op jit(solution)/shard_map/slice | solution.py:15
  152.9 4.1 %copy.8 = bf16[32,2,192,32]{2,3,1,0:T(8,128)(2,1)} copy(bf16[32,2,192,32]{3,2,1,0:T(8,128)(2,1)} %get-tuple-element.176) | data formatting | bytes 1572864 | tf_op jit(solution)/shard_map/slice | solution.py:15
  157.0 3.4 %collective-permute-start.6 = (bf16[32,2,192,32]{2,3,1,0:T(8,128)(2,1)}, bf16[32,2,192,32]{2,3,1,0:T(8,128)(2,1)}, u32[]{:S(2)}, u32[]{:S(2)}) collective-permute-start(bf16[32,2,192,32]{2,3,1,0:T(8,128)(2,1)} %copy.8), channel_id=1, source_target_pairs={{0,32},{1,33},{2,34},{3,35},{4,36},{5,37},{6,38},{7,39},{8,40},{9,... | collective-permute-start | bytes 2359304 | tf_op jit(solution)/shard_map/ppermute | solution.py:18
  160.4 3.0 copy.9
  164.9 16.5 %collective-permute-done.6 = bf16[32,2,192,32]{2,3,1,0:T(8,128)(2,1)} collective-permute-done((bf16[32,2,192,32]{2,3,1,0:T(8,128)(2,1)}, bf16[32,2,192,32]{2,3,1,0:T(8,128)(2,1)}, u32[]{:S(2)}, u32[]{:S(2)}) %collective-permute-start.6) | collective-permute-done | bytes 786464 | tf_op jit(solution)/shard_map/ppermute | solution.py:18
  181.4 3.4 %copy.10 = bf16[32,2,192,32]{3,2,1,0:T(8,128)(2,1)S(1)} copy(bf16[32,2,192,32]{2,3,1,0:T(8,128)(2,1)} %collective-permute-done.6) | data formatting | bytes 1572864 | tf_op jit(solution)/shard_map/ppermute | solution.py:18
  184.8 4.7 %collective-permute-done.7 = bf16[32,2,192,32]{2,3,1,0:T(8,128)(2,1)} collective-permute-done((bf16[32,2,192,32]{2,3,1,0:T(8,128)(2,1)}, bf16[32,2,192,32]{2,3,1,0:T(8,128)(2,1)}, u32[]{:S(2)}, u32[]{:S(2)}) %collective-permute-start.7) | collective-permute-done | bytes 786464 | tf_op jit(solution)/shard_map/ppermute | solution.py:20
  189.5 3.9 %copy.11 = bf16[32,2,192,32]{3,2,1,0:T(8,128)(2,1)} copy(bf16[32,2,192,32]{2,3,1,0:T(8,128)(2,1)} %collective-permute-done.7) | data formatting | bytes 1572864 | tf_op jit(solution)/shard_map/ppermute | solution.py:20
  193.4 11.6 %pad_maximum_fusion = bf16[32,2,192,320]{3,2,1,0:T(8,128)(2,1)} fusion(bf16[32,2,192,32]{3,2,1,0:T(8,128)(2,1)} %copy.11, bf16[32,2,192,256]{3,2,1,0:T(8,128)(2,1)} %copy-done, bf16[32,2,192,32]{3,2,1,0:T(8,128)(2,1)S(1)} %copy.10), kind=kLoop, calls=%fused_computation.117 | loop fusion | flops 23592960 | bytes 15728640 | tf_op jit(solution)/shard_map/concatenate | solution.py:16
  205.0 106.6 %while.15 = (s32[]{:T(128)}, f32[6,2,128,256]{3,2,0,1:T(8,128)}, s32[6,2]{0,1:T(2,128)S(1)}, s32[32]{0:T(128)S(1)}, bf16[32,2,192,320]{3,2,1,0:T(8,128)(2,1)}, /*index=5*/s32[]{:T(128)}) while((s32[]{:T(128)}, f32[6,2,128,256]{3,2,0,1:T(8,128)}, s32[6,2]{0,1:T(2,128)S(1)}, s32[32]{0:T(128)S(1)}, bf16[32,2,192,320]{3,2,1,0:T(8,128)(2,1)}, ...), condition=%wide.region_2.3_spmd, body=%wide.region_1.2_spmd.sunk | while | flops 2396370688 | bytes 19467128 | solution.py:84
  208.3 7.6 %fusion.178 = bf16[32,2,128,320]{2,3,0,1:T(8,128)(2,1)S(1)} fusion(bf16[32,2,192,320]{3,2,1,0:T(8,128)(2,1)} %get-tuple-element.288, s32[32]{0:T(128)S(1)} %get-tuple-element.267, s32[128,192]{1,0:T(8,128)S(1)} %iota_subtract_fusion.5, bf16[32]{0:T(256)(128)(2,1)S(1)} %get-tuple-element.268, ...), kind=kOutput, calls=%fused_computation.19.clone.clone.clone.clone.clone.2.clone.1 | convolution fusion | flops 1022623744 | bytes 13205888 | tf_op jit(solution)/shard_map/while/body/eval_jaxpr/erp,eipk->eirk/dot_general | solution.py:79
  215.9 6.9 %fusion.179 = f32[6,2,128,256]{3,2,0,1:T(8,128)} fusion(f32[6,2,128,256]{3,2,0,1:T(8,128)} %get-tuple-element.279, s32[]{:T(128)} %get-tuple-element.278, s32[32]{0:T(128)S(1)} %get-tuple-element.260, s32[256,320]{0,1:T(8,128)S(1)} %iota_subtract_fusion.4, bf16[32]{0:T(256)(128)(2,1)S(1)} %get-tuple-element.263, ...), kind=kOutput, calls=%fused_computation.47.clone.3 | convolution fusion | flops 1373634560 | bytes 5833600 | tf_op jit(solution)/shard_map/while/body/eval_jaxpr/eirk,eck->irc/dot_general | solution.py:82
  226.1 7.6 %fusion.178 = bf16[32,2,128,320]{2,3,0,1:T(8,128)(2,1)S(1)} fusion(bf16[32,2,192,320]{3,2,1,0:T(8,128)(2,1)} %get-tuple-element.288, s32[32]{0:T(128)S(1)} %get-tuple-element.267, s32[128,192]{1,0:T(8,128)S(1)} %iota_subtract_fusion.5, bf16[32]{0:T(256)(128)(2,1)S(1)} %get-tuple-element.268, ...), kind=kOutput, calls=%fused_computation.19.clone.clone.clone.clone.clone.2.clone.1 | convolution fusion | flops 1022623744 | bytes 13205888 | tf_op jit(solution)/shard_map/while/body/eval_jaxpr/erp,eipk->eirk/dot_general | solution.py:79
  233.7 6.9 %fusion.179 = f32[6,2,128,256]{3,2,0,1:T(8,128)} fusion(f32[6,2,128,256]{3,2,0,1:T(8,128)} %get-tuple-element.279, s32[]{:T(128)} %get-tuple-element.278, s32[32]{0:T(128)S(1)} %get-tuple-element.260, s32[256,320]{0,1:T(8,128)S(1)} %iota_subtract_fusion.4, bf16[32]{0:T(256)(128)(2,1)S(1)} %get-tuple-element.263, ...), kind=kOutput, calls=%fused_computation.47.clone.3 | convolution fusion | flops 1373634560 | bytes 5833600 | tf_op jit(solution)/shard_map/while/body/eval_jaxpr/eirk,eck->irc/dot_general | solution.py:82
  243.8 7.6 %fusion.178 = bf16[32,2,128,320]{2,3,0,1:T(8,128)(2,1)S(1)} fusion(bf16[32,2,192,320]{3,2,1,0:T(8,128)(2,1)} %get-tuple-element.288, s32[32]{0:T(128)S(1)} %get-tuple-element.267, s32[128,192]{1,0:T(8,128)S(1)} %iota_subtract_fusion.5, bf16[32]{0:T(256)(128)(2,1)S(1)} %get-tuple-element.268, ...), kind=kOutput, calls=%fused_computation.19.clone.clone.clone.clone.clone.2.clone.1 | convolution fusion | flops 1022623744 | bytes 13205888 | tf_op jit(solution)/shard_map/while/body/eval_jaxpr/erp,eipk->eirk/dot_general | solution.py:79
  251.5 6.9 %fusion.179 = f32[6,2,128,256]{3,2,0,1:T(8,128)} fusion(f32[6,2,128,256]{3,2,0,1:T(8,128)} %get-tuple-element.279, s32[]{:T(128)} %get-tuple-element.278, s32[32]{0:T(128)S(1)} %get-tuple-element.260, s32[256,320]{0,1:T(8,128)S(1)} %iota_subtract_fusion.4, bf16[32]{0:T(256)(128)(2,1)S(1)} %get-tuple-element.263, ...), kind=kOutput, calls=%fused_computation.47.clone.3 | convolution fusion | flops 1373634560 | bytes 5833600 | tf_op jit(solution)/shard_map/while/body/eval_jaxpr/eirk,eck->irc/dot_general | solution.py:82
  261.6 7.6 %fusion.178 = bf16[32,2,128,320]{2,3,0,1:T(8,128)(2,1)S(1)} fusion(bf16[32,2,192,320]{3,2,1,0:T(8,128)(2,1)} %get-tuple-element.288, s32[32]{0:T(128)S(1)} %get-tuple-element.267, s32[128,192]{1,0:T(8,128)S(1)} %iota_subtract_fusion.5, bf16[32]{0:T(256)(128)(2,1)S(1)} %get-tuple-element.268, ...), kind=kOutput, calls=%fused_computation.19.clone.clone.clone.clone.clone.2.clone.1 | convolution fusion | flops 1022623744 | bytes 13205888 | tf_op jit(solution)/shard_map/while/body/eval_jaxpr/erp,eipk->eirk/dot_general | solution.py:79
  269.2 6.9 %fusion.179 = f32[6,2,128,256]{3,2,0,1:T(8,128)} fusion(f32[6,2,128,256]{3,2,0,1:T(8,128)} %get-tuple-element.279, s32[]{:T(128)} %get-tuple-element.278, s32[32]{0:T(128)S(1)} %get-tuple-element.260, s32[256,320]{0,1:T(8,128)S(1)} %iota_subtract_fusion.4, bf16[32]{0:T(256)(128)(2,1)S(1)} %get-tuple-element.263, ...), kind=kOutput, calls=%fused_computation.47.clone.3 | convolution fusion | flops 1373634560 | bytes 5833600 | tf_op jit(solution)/shard_map/while/body/eval_jaxpr/eirk,eck->irc/dot_general | solution.py:82
  279.4 7.6 %fusion.178 = bf16[32,2,128,320]{2,3,0,1:T(8,128)(2,1)S(1)} fusion(bf16[32,2,192,320]{3,2,1,0:T(8,128)(2,1)} %get-tuple-element.288, s32[32]{0:T(128)S(1)} %get-tuple-element.267, s32[128,192]{1,0:T(8,128)S(1)} %iota_subtract_fusion.5, bf16[32]{0:T(256)(128)(2,1)S(1)} %get-tuple-element.268, ...), kind=kOutput, calls=%fused_computation.19.clone.clone.clone.clone.clone.2.clone.1 | convolution fusion | flops 1022623744 | bytes 13205888 | tf_op jit(solution)/shard_map/while/body/eval_jaxpr/erp,eipk->eirk/dot_general | solution.py:79
  287.0 6.9 %fusion.179 = f32[6,2,128,256]{3,2,0,1:T(8,128)} fusion(f32[6,2,128,256]{3,2,0,1:T(8,128)} %get-tuple-element.279, s32[]{:T(128)} %get-tuple-element.278, s32[32]{0:T(128)S(1)} %get-tuple-element.260, s32[256,320]{0,1:T(8,128)S(1)} %iota_subtract_fusion.4, bf16[32]{0:T(256)(128)(2,1)S(1)} %get-tuple-element.263, ...), kind=kOutput, calls=%fused_computation.47.clone.3 | convolution fusion | flops 1373634560 | bytes 5833600 | tf_op jit(solution)/shard_map/while/body/eval_jaxpr/eirk,eck->irc/dot_general | solution.py:82
  297.1 7.6 %fusion.178 = bf16[32,2,128,320]{2,3,0,1:T(8,128)(2,1)S(1)} fusion(bf16[32,2,192,320]{3,2,1,0:T(8,128)(2,1)} %get-tuple-element.288, s32[32]{0:T(128)S(1)} %get-tuple-element.267, s32[128,192]{1,0:T(8,128)S(1)} %iota_subtract_fusion.5, bf16[32]{0:T(256)(128)(2,1)S(1)} %get-tuple-element.268, ...), kind=kOutput, calls=%fused_computation.19.clone.clone.clone.clone.clone.2.clone.1 | convolution fusion | flops 1022623744 | bytes 13205888 | tf_op jit(solution)/shard_map/while/body/eval_jaxpr/erp,eipk->eirk/dot_general | solution.py:79
  304.8 6.9 %fusion.179 = f32[6,2,128,256]{3,2,0,1:T(8,128)} fusion(f32[6,2,128,256]{3,2,0,1:T(8,128)} %get-tuple-element.279, s32[]{:T(128)} %get-tuple-element.278, s32[32]{0:T(128)S(1)} %get-tuple-element.260, s32[256,320]{0,1:T(8,128)S(1)} %iota_subtract_fusion.4, bf16[32]{0:T(256)(128)(2,1)S(1)} %get-tuple-element.263, ...), kind=kOutput, calls=%fused_computation.47.clone.3 | convolution fusion | flops 1373634560 | bytes 5833600 | tf_op jit(solution)/shard_map/while/body/eval_jaxpr/eirk,eck->irc/dot_general | solution.py:82
  (76 shorter events, 43.5 us)
Async XLA Ops:
  6.5 110.4 %all-gather.2.cloned.1.call-start = ((), (), s32[]{:S(2)}) async-start(), calls=%async_computation | async-start | bytes 4325376 | tf_op jit(solution)/shard_map/all_gather | solution.py:97
  8.2 8.4 %collective-permute-start = (f32[2,1,4,256]{3,2,1,0:T(4,128)S(1)}, f32[2,1,4,256]{3,2,1,0:T(4,128)S(1)}, u32[]{:S(2)}, u32[]{:S(2)}) collective-permute-start(f32[2,1,4,256]{3,2,1,0:T(4,128)S(1)} %get-tuple-element.184), channel_id=1, source_target_pairs={{0,64},{64,128},{128,192},{1,65},{65,129},{129,193},{2,66},{66,130... | collective-permute-start | bytes 24584 | tf_op jit(solution)/shard_map/ppermute | solution.py:18
  11.7 5.5 %collective-permute-start.1 = (f32[2,1,4,256]{3,2,1,0:T(4,128)S(1)}, f32[2,1,4,256]{3,2,1,0:T(4,128)S(1)}, u32[]{:S(2)}, u32[]{:S(2)}) collective-permute-start(f32[2,1,4,256]{3,2,1,0:T(4,128)S(1)} %get-tuple-element.185), channel_id=1, source_target_pairs={{64,0},{128,64},{192,128},{65,1},{129,65},{193,129},{66,2},{130,66... | collective-permute-start | bytes 24584 | tf_op jit(solution)/shard_map/ppermute | solution.py:20
  18.3 6.4 %collective-permute-start.2 = (f32[2,1,136,4]{3,2,1,0:T(8,128)S(1)}, f32[2,1,136,4]{3,2,1,0:T(8,128)S(1)}, u32[]{:S(2)}, u32[]{:S(2)}) collective-permute-start(f32[2,1,136,4]{3,2,1,0:T(8,128)S(1)} %get-tuple-element.182), channel_id=1, source_target_pairs={{0,32},{1,33},{2,34},{3,35},{4,36},{5,37},{6,38},{7,39},{8,40},{9,... | collective-permute-start | bytes 13064 | tf_op jit(solution)/shard_map/ppermute | solution.py:18
  22.1 6.9 %collective-permute-start.3 = (f32[2,1,136,4]{3,2,1,0:T(8,128)S(1)}, f32[2,1,136,4]{3,2,1,0:T(8,128)S(1)}, u32[]{:S(2)}, u32[]{:S(2)}) collective-permute-start(f32[2,1,136,4]{3,2,1,0:T(8,128)S(1)} %get-tuple-element.183), channel_id=1, source_target_pairs={{32,0},{33,1},{34,2},{35,3},{36,4},{37,5},{38,6},{39,7},{40,8},{41... | collective-permute-start | bytes 13064 | tf_op jit(solution)/shard_map/ppermute | solution.py:20
  116.9 29.2 %copy-start.1 = (bf16[32,2,128,256]{3,2,1,0:T(8,128)(2,1)S(1)}, bf16[32,2,128,256]{3,2,1,0:T(8,128)(2,1)}, u32[]{:S(2)}) copy-start(bf16[32,2,128,256]{3,2,1,0:T(8,128)(2,1)} %all-gather.2.cloned.1.call-done) | copy-start | bytes 12582916
  118.8 27.2 %collective-permute-start.4 = (bf16[32,2,32,256]{3,2,1,0:T(8,128)(2,1)S(1)}, bf16[32,2,32,256]{3,2,1,0:T(8,128)(2,1)S(1)}, u32[]{:S(2)}, u32[]{:S(2)}) collective-permute-start(bf16[32,2,32,256]{3,2,1,0:T(8,128)(2,1)S(1)} %get-tuple-element.179), channel_id=1, source_target_pairs={{0,64},{64,128},{128,192},{1,65},{65,129},{129,193},{2,66},{66,130... | collective-permute-start | bytes 3145736 | tf_op jit(solution)/shard_map/ppermute | solution.py:18
  122.2 26.9 %collective-permute-start.5 = (bf16[32,2,32,256]{3,2,1,0:T(8,128)(2,1)S(1)}, bf16[32,2,32,256]{3,2,1,0:T(8,128)(2,1)S(1)}, u32[]{:S(2)}, u32[]{:S(2)}) collective-permute-start(bf16[32,2,32,256]{3,2,1,0:T(8,128)(2,1)S(1)} %get-tuple-element.178), channel_id=1, source_target_pairs={{64,0},{128,64},{192,128},{65,1},{129,65},{193,129},{66,2},{130,66... | collective-permute-start | bytes 3145736 | tf_op jit(solution)/shard_map/ppermute | solution.py:20
  149.2 3.7 %copy-start = (bf16[32,2,192,256]{3,2,1,0:T(8,128)(2,1)}, bf16[32,2,192,256]{3,2,1,0:T(8,128)(2,1)S(1)}, u32[]{:S(2)}) copy-start(bf16[32,2,192,256]{3,2,1,0:T(8,128)(2,1)S(1)} %constant_dynamic-update-slice_fusion) | copy-start | bytes 18874372
  157.0 24.4 %collective-permute-start.6 = (bf16[32,2,192,32]{2,3,1,0:T(8,128)(2,1)}, bf16[32,2,192,32]{2,3,1,0:T(8,128)(2,1)}, u32[]{:S(2)}, u32[]{:S(2)}) collective-permute-start(bf16[32,2,192,32]{2,3,1,0:T(8,128)(2,1)} %copy.8), channel_id=1, source_target_pairs={{0,32},{1,33},{2,34},{3,35},{4,36},{5,37},{6,38},{7,39},{8,40},{9,... | collective-permute-start | bytes 2359304 | tf_op jit(solution)/shard_map/ppermute | solution.py:18
  163.4 26.1 %collective-permute-start.7 = (bf16[32,2,192,32]{2,3,1,0:T(8,128)(2,1)}, bf16[32,2,192,32]{2,3,1,0:T(8,128)(2,1)}, u32[]{:S(2)}, u32[]{:S(2)}) collective-permute-start(bf16[32,2,192,32]{2,3,1,0:T(8,128)(2,1)} %copy.9), channel_id=1, source_target_pairs={{32,0},{33,1},{34,2},{35,3},{36,4},{37,5},{38,6},{39,7},{40,8},{41... | collective-permute-start | bytes 2359304 | tf_op jit(solution)/shard_map/ppermute | solution.py:20
  193.4 11.6 %copy-start.2 = (s32[32]{0:T(128)S(1)}, s32[32]{0:T(128)}, u32[]{:S(2)}) copy-start(s32[32]{0:T(128)} %param.10) | copy-start | bytes 388
  193.4 11.6 %copy-start.3 = (s32[6,2]{0,1:T(2,128)S(1)}, s32[6,2]{0,1:T(2,128)}, u32[]{:S(2)}) copy-start(s32[6,2]{0,1:T(2,128)} %param.11) | copy-start | bytes 148
Sparse Core Ops, SparseCore 0:
  54.8 61.9 all-gather.1
where the time goes:
time: 322 us; the launch traced here: 321 us
  waiting for transfers between devices  113 us (35%)
  matrix products  86.9 us (27%)
  other arithmetic  60.5 us (19%)
  local copies, waits for them, and re-layouts  25 us (8%)
  starting transfers between devices  21.7 us (7%)
  between operations  13.6 us (4%)
    all_gather x1, waiting for transfers between devices, shards(): every_epoch = lax.all_gather(images, 'ea', axis=0, tiled=True)  62.2 us
    dot_general x6, matrix products, one_hyp(): jnp.einsum('erp,eipk->eirk', row_band, padded, preferred_element_type=jnp...  45.7 us
    dot_general x6, matrix products, one_hyp(): jnp.einsum('eirk,eck->irc', moved_rows, col_band, preferred_element_type=...  41.3 us
    ppermute x4, waiting for transfers between devices, extended(): lax.ppermute(tail, axis, [(i, (i + 1) % count) for i in range(ends)])  38.4 us
    ppermute x4, starting transfers between devices, extended(): lax.ppermute(tail, axis, [(i, (i + 1) % count) for i in range(ends)])  14.1 us
    concatenate x3, other arithmetic, extended(): jnp.concatenate([lax.ppermute(tail, axis, [(i, (i + 1) % count) for i in...  13.7 us
    another operation x3, other arithmetic, shards(): images = jnp.stack([psi, phi], 1)  12.7 us
    ppermute x4, waiting for transfers between devices, extended(): lax.ppermute(head, axis, [((i + 1) % count, i) for i in range(ends)])  12.4 us
  transfers between devices with their start and end apart: 9, of which 8 were waited for; matrix products, arithmetic and copies ran while one was open for 3% of the time, Pallas kernels for 0%

commit v1 on v0

--- a/solution.py
+++ b/solution.py
@@ -2,6 +2,7 @@
 import jax.numpy as jnp
 from jax import lax
 from jax.sharding import PartitionSpec as P
+from jax.lax import all_to_all, axis_size
 
 REACH = 32
 PR = 4
@@ -94,7 +95,15 @@
     psi = blur(framed[0], kern_p).astype(jnp.bfloat16)
     phi = blur(framed[1], kern_q).astype(jnp.bfloat16)
     images = jnp.stack([psi, phi], 1)
-    every_epoch = lax.all_gather(images, "ea", axis=0, tiled=True)
+    every_epoch = jnp.concatenate(
+        all_to_all(
+            jnp.stack([images for _ in range(axis_size("ea"))], axis=0),
+            split_axis=0,
+            axis_name="ea",
+            concat_axis=0,
+        ),
+        axis=0,
+    )
     padded = extended(every_epoch, (("tx", 2), ("ty", 3)), REACH)
     stacks = stack_block(padded, epoch_times, velocities, out_rows, out_cols)
     return stacks[:, 0] / jnp.sqrt(stacks[:, 1])

time: 322 us -> 353 us (1.096)
  blocking collectives: 0 us -> 106 us
  waiting for transfers between devices: 113 us -> 50.3 us
  between operations: 13.6 us -> 0.17 us
    all_to_all x0 -> x1, blocking collectives: none -> 106 us  [shards(): all_to_all(jnp.stack([images for _ in range(axis_size('ea'))], axis=0), s...]
    all_gather x1 -> x0, waiting for transfers between devices: 62.2 us -> none  [shards(): every_epoch = lax.all_gather(images, 'ea', axis=0, tiled=True)]
    concatenate x3 -> x4, other arithmetic: 13.7 us -> 17.8 us  [extended(): jnp.concatenate([lax.ppermute(tail, axis, [(i, (i + 1) % count) for i in...]
    slice x3 -> x4, local copies, waits for them, and re-layouts: 7.89 us -> 7.61 us  [extended(): lax.slice_in_dim(cells, cells.shape[dim] - width, cells.shape[dim], axis=...]
  transfers between devices with their start and end apart: 9 -> 8, of which waited for: 8 -> 7; matrix products, arithmetic and copies ran while one was open for 3% -> 3% of each run, Pallas kernels for 0% -> 0%
where the time goes in v1:
time: 353 us; the launch traced here: 351 us
  blocking collectives  106 us (30%)
  matrix products  86.9 us (25%)
  other arithmetic  63.1 us (18%)
  waiting for transfers between devices  50.3 us (14%)
  local copies, waits for them, and re-layouts  23.7 us (7%)
  starting transfers between devices  20.6 us (6%)
    all_to_all x1, blocking collectives, shards(): all_to_all(jnp.stack([images for _ in range(axis_size('ea'))], axis=0), s...  106 us
    dot_general x6, matrix products, one_hyp(): jnp.einsum('erp,eipk->eirk', row_band, padded, preferred_element_type=jnp...  45.6 us
    dot_general x6, matrix products, one_hyp(): jnp.einsum('eirk,eck->irc', moved_rows, col_band, preferred_element_type=...  41.2 us
    ppermute x4, waiting for transfers between devices, extended(): lax.ppermute(tail, axis, [(i, (i + 1) % count) for i in range(ends)])  37.8 us
    concatenate x4, other arithmetic, extended(): jnp.concatenate([lax.ppermute(tail, axis, [(i, (i + 1) % count) for i in...  17.8 us
    ppermute x4, starting transfers between devices, extended(): lax.ppermute(tail, axis, [(i, (i + 1) % count) for i in range(ends)])  12.7 us
    ppermute x4, waiting for transfers between devices, extended(): lax.ppermute(head, axis, [((i + 1) % count, i) for i in range(ends)])  12.6 us
    another operation x3, other arithmetic, shards(): images = jnp.stack([psi, phi], 1)  12 us
  transfers between devices with their start and end apart: 8, of which 7 were waited for; matrix products, arithmetic and copies ran while one was open for 3% of the time, Pallas kernels for 0%

profile of v1, /device:TPU:8, one launch (start us, length us, event | category | flops | bytes accessed | tf_op | source)
XLA Modules:
  0.0 351.3 jit_solution(2062053520824853920)
XLA Ops:
  1.7 3.5 collective-permute-start
  11.8 3.8 %collective-permute-start.2 = (f32[2,1,136,4]{3,2,1,0:T(8,128)S(1)}, f32[2,1,136,4]{3,2,1,0:T(8,128)S(1)}, u32[]{:S(2)}, u32[]{:S(2)}) collective-permute-start(f32[2,1,136,4]{3,2,1,0:T(8,128)S(1)} %get-tuple-element.182), channel_id=1, source_target_pairs={{0,32},{1,33},{2,34},{3,35},{4,36},{5,37},{6,38},{7,39},{8,40},{9,... | collective-permute-start | bytes 13064 | tf_op jit(solution)/shard_map/ppermute | solution.py:19
  18.2 4.4 %collective-permute-done.3 = f32[2,1,136,4]{3,2,1,0:T(8,128)S(1)} collective-permute-done((f32[2,1,136,4]{3,2,1,0:T(8,128)S(1)}, f32[2,1,136,4]{3,2,1,0:T(8,128)S(1)}, u32[]{:S(2)}, u32[]{:S(2)}) %collective-permute-start.3) | collective-permute-done | bytes 4384 | tf_op jit(solution)/shard_map/ppermute | solution.py:21
  23.7 6.0 %fusion.111 = f32[1,128,264]{2,1,0:T(8,128)S(1)} fusion(f32[1,136,264]{2,1,0:T(8,128)S(1)} %get-tuple-element.180, f32[]{:T(128)} %bitcast.29, f32[]{:T(128)} %bitcast.28, f32[]{:T(128)} %bitcast.27, f32[]{:T(128)} %bitcast.26, f32[]{:T(128)} %bitcast.25, f32[]{:T(128)} %bitcast.24, f32[]{:T(128)} %bitcast.23, f32[]{:T(128)} %bitcast.22, f32[]{:T(128)} %bitcast.18), kind=kLoop, calls=%fused_computation.142 | loop fusion | flops 574464 | bytes 1351716 | tf_op jit(solution)/shard_map/add | solution.py:33
  29.7 6.1 %fusion.137 = bf16[1,1,128,256]{3,2,1,0:T(8,128)(2,1)S(1)} fusion(f32[1,128,264]{2,1,0:T(8,128)S(1)} %fusion.111, f32[]{:T(128)} %bitcast.29, f32[]{:T(128)} %bitcast.28, f32[]{:T(128)} %bitcast.27, f32[]{:T(128)} %bitcast.26, f32[]{:T(128)} %bitcast.25, f32[]{:T(128)} %bitcast.24, f32[]{:T(128)} %bitcast.23, f32[]{:T(128)} %bitcast.22, f32[]{:T(128)} %bitcast.18), kind=kLoop, calls=%fused_computation.196 | loop fusion | flops 589824 | bytes 1245220 | tf_op jit(solution)/shard_map/stack | solution.py:97
  35.8 5.8 %fusion.103 = f32[1,128,264]{2,1,0:T(8,128)S(1)} fusion(f32[1,136,264]{2,1,0:T(8,128)S(1)} %get-tuple-element.181, f32[]{:T(128)} %bitcast.40, f32[]{:T(128)} %bitcast.39, f32[]{:T(128)} %bitcast.38, f32[]{:T(128)} %bitcast.37, f32[]{:T(128)} %bitcast.36, f32[]{:T(128)} %bitcast.35, f32[]{:T(128)} %bitcast.34, f32[]{:T(128)} %bitcast.33, f32[]{:T(128)} %bitcast.31), kind=kLoop, calls=%fused_computation.125 | loop fusion | flops 574464 | bytes 1351716 | tf_op jit(solution)/shard_map/add | solution.py:33
  41.6 5.9 %fusion.138 = bf16[1,1,128,256]{3,2,1,0:T(8,128)(2,1)S(1)} fusion(f32[1,128,264]{2,1,0:T(8,128)S(1)} %fusion.103, f32[]{:T(128)} %bitcast.40, f32[]{:T(128)} %bitcast.39, f32[]{:T(128)} %bitcast.38, f32[]{:T(128)} %bitcast.37, f32[]{:T(128)} %bitcast.36, f32[]{:T(128)} %bitcast.35, f32[]{:T(128)} %bitcast.34, f32[]{:T(128)} %bitcast.33, f32[]{:T(128)} %bitcast.31), kind=kLoop, calls=%fused_computation.197 | loop fusion | flops 589824 | bytes 1245220 | tf_op jit(solution)/shard_map/stack | solution.py:97
  48.0 106.3 %all_to_all.5 = bf16[32,1,2,128,256]{4,3,2,1,0:T(8,128)(2,1)S(1)} all-to-all(bf16[32,1,2,128,256]{4,3,2,1,0:T(8,128)(2,1)S(1)} %stack.39), channel_id=1, replica_groups=mesh['tx'=4,'ty'=2,'ea'=32] {'ea'}, dimensions={0} | all-to-all | bytes 8388608 | tf_op jit(solution)/shard_map/all_to_all | solution.py:99
  154.6 3.2 collective-permute-start.4
  160.5 20.9 %collective-permute-done.4 = bf16[32,2,32,256]{3,2,1,0:T(8,128)(2,1)S(1)} collective-permute-done((bf16[32,2,32,256]{3,2,1,0:T(8,128)(2,1)S(1)}, bf16[32,2,32,256]{3,2,1,0:T(8,128)(2,1)S(1)}, u32[]{:S(2)}, u32[]{:S(2)}) %collective-permute-start.4) | collective-permute-done | bytes 1048608 | tf_op jit(solution)/shard_map/ppermute | solution.py:19
  185.2 4.2 %pad_maximum_fusion.1 = bf16[32,2,192,256]{3,2,1,0:T(8,128)(2,1)S(1)} fusion(bf16[32,2,32,256]{3,2,1,0:T(8,128)(2,1)S(1)} %collective-permute-done.5, bf16[32,2,128,256]{3,2,1,0:T(8,128)(2,1)S(1)} %bitcast.137, bf16[32,2,32,256]{3,2,1,0:T(8,128)(2,1)S(1)} %collective-permute-done.4), kind=kLoop, calls=%fused_computation.118 | loop fusion | flops 18874368 | bytes 12582912 | tf_op jit(solution)/shard_map/concatenate | solution.py:17
  189.4 3.2 fusion.141
  192.6 4.2 %copy.8 = bf16[32,2,192,32]{2,3,1,0:T(8,128)(2,1)} copy(bf16[32,2,192,32]{3,2,1,0:T(8,128)(2,1)} %get-tuple-element.176) | data formatting | bytes 1572864 | tf_op jit(solution)/shard_map/slice | solution.py:16
  199.0 3.0 copy.9
  203.5 16.3 %collective-permute-done.6 = bf16[32,2,192,32]{2,3,1,0:T(8,128)(2,1)} collective-permute-done((bf16[32,2,192,32]{2,3,1,0:T(8,128)(2,1)}, bf16[32,2,192,32]{2,3,1,0:T(8,128)(2,1)}, u32[]{:S(2)}, u32[]{:S(2)}) %collective-permute-start.6) | collective-permute-done | bytes 786464 | tf_op jit(solution)/shard_map/ppermute | solution.py:19
  219.9 3.4 copy.10
  223.3 4.7 %collective-permute-done.7 = bf16[32,2,192,32]{2,3,1,0:T(8,128)(2,1)} collective-permute-done((bf16[32,2,192,32]{2,3,1,0:T(8,128)(2,1)}, bf16[32,2,192,32]{2,3,1,0:T(8,128)(2,1)}, u32[]{:S(2)}, u32[]{:S(2)}) %collective-permute-start.7) | collective-permute-done | bytes 786464 | tf_op jit(solution)/shard_map/ppermute | solution.py:21
  227.9 3.9 %copy.11 = bf16[32,2,192,32]{3,2,1,0:T(8,128)(2,1)} copy(bf16[32,2,192,32]{2,3,1,0:T(8,128)(2,1)} %collective-permute-done.7) | data formatting | bytes 1572864 | tf_op jit(solution)/shard_map/ppermute | solution.py:21
  231.8 11.6 %pad_maximum_fusion = bf16[32,2,192,320]{3,2,1,0:T(8,128)(2,1)} fusion(bf16[32,2,192,32]{3,2,1,0:T(8,128)(2,1)} %copy.11, bf16[32,2,32,256]{3,2,1,0:T(8,128)(2,1)} %copy-done.2, bf16[32,2,128,256]{3,2,1,0:T(8,128)(2,1)} %bitcast.138, bf16[32,2,32,256]{3,2,1,0:T(8,128)(2,1)} %copy-done.1, bf16[32,2,192,32]{3,2,1,0:T(8,128)(2,1)S(1)} %copy.10), kind=kLoop, calls=%fused_computation.117 | loop fusion | flops 39321600 | bytes 15728640 | tf_op jit(solution)/shard_map/concatenate | solution.py:17
  243.4 105.6 %while.15 = (s32[]{:T(128)}, f32[6,2,128,256]{3,2,0,1:T(8,128)}, s32[6,2]{0,1:T(2,128)S(1)}, s32[32]{0:T(128)S(1)}, bf16[32,2,192,320]{3,2,1,0:T(8,128)(2,1)}, /*index=5*/s32[]{:T(128)}) while((s32[]{:T(128)}, f32[6,2,128,256]{3,2,0,1:T(8,128)}, s32[6,2]{0,1:T(2,128)S(1)}, s32[32]{0:T(128)S(1)}, bf16[32,2,192,320]{3,2,1,0:T(8,128)(2,1)}, ...), condition=%wide.region_2.3_spmd, body=%wide.region_1.2_spmd.sunk | while | flops 2396370688 | bytes 19467128 | solution.py:85
  246.5 7.6 %fusion.178 = bf16[32,2,128,320]{2,3,0,1:T(8,128)(2,1)S(1)} fusion(bf16[32,2,192,320]{3,2,1,0:T(8,128)(2,1)} %get-tuple-element.288, s32[32]{0:T(128)S(1)} %get-tuple-element.267, s32[128,192]{1,0:T(8,128)S(1)} %iota_subtract_fusion.5, bf16[32]{0:T(256)(128)(2,1)S(1)} %get-tuple-element.268, ...), kind=kOutput, calls=%fused_computation.19.clone.clone.clone.clone.clone.2.clone.1 | convolution fusion | flops 1022623744 | bytes 13205888 | tf_op jit(solution)/shard_map/while/body/eval_jaxpr/erp,eipk->eirk/dot_general | solution.py:80
  254.1 6.9 %fusion.179 = f32[6,2,128,256]{3,2,0,1:T(8,128)} fusion(f32[6,2,128,256]{3,2,0,1:T(8,128)} %get-tuple-element.279, s32[]{:T(128)} %get-tuple-element.278, s32[32]{0:T(128)S(1)} %get-tuple-element.260, s32[256,320]{0,1:T(8,128)S(1)} %iota_subtract_fusion.4, bf16[32]{0:T(256)(128)(2,1)S(1)} %get-tuple-element.263, ...), kind=kOutput, calls=%fused_computation.47.clone.3 | convolution fusion | flops 1373634560 | bytes 5833600 | tf_op jit(solution)/shard_map/while/body/eval_jaxpr/eirk,eck->irc/dot_general | solution.py:83
  264.1 7.6 %fusion.178 = bf16[32,2,128,320]{2,3,0,1:T(8,128)(2,1)S(1)} fusion(bf16[32,2,192,320]{3,2,1,0:T(8,128)(2,1)} %get-tuple-element.288, s32[32]{0:T(128)S(1)} %get-tuple-element.267, s32[128,192]{1,0:T(8,128)S(1)} %iota_subtract_fusion.5, bf16[32]{0:T(256)(128)(2,1)S(1)} %get-tuple-element.268, ...), kind=kOutput, calls=%fused_computation.19.clone.clone.clone.clone.clone.2.clone.1 | convolution fusion | flops 1022623744 | bytes 13205888 | tf_op jit(solution)/shard_map/while/body/eval_jaxpr/erp,eipk->eirk/dot_general | solution.py:80
  271.7 6.9 %fusion.179 = f32[6,2,128,256]{3,2,0,1:T(8,128)} fusion(f32[6,2,128,256]{3,2,0,1:T(8,128)} %get-tuple-element.279, s32[]{:T(128)} %get-tuple-element.278, s32[32]{0:T(128)S(1)} %get-tuple-element.260, s32[256,320]{0,1:T(8,128)S(1)} %iota_subtract_fusion.4, bf16[32]{0:T(256)(128)(2,1)S(1)} %get-tuple-element.263, ...), kind=kOutput, calls=%fused_computation.47.clone.3 | convolution fusion | flops 1373634560 | bytes 5833600 | tf_op jit(solution)/shard_map/while/body/eval_jaxpr/eirk,eck->irc/dot_general | solution.py:83
  281.7 7.6 %fusion.178 = bf16[32,2,128,320]{2,3,0,1:T(8,128)(2,1)S(1)} fusion(bf16[32,2,192,320]{3,2,1,0:T(8,128)(2,1)} %get-tuple-element.288, s32[32]{0:T(128)S(1)} %get-tuple-element.267, s32[128,192]{1,0:T(8,128)S(1)} %iota_subtract_fusion.5, bf16[32]{0:T(256)(128)(2,1)S(1)} %get-tuple-element.268, ...), kind=kOutput, calls=%fused_computation.19.clone.clone.clone.clone.clone.2.clone.1 | convolution fusion | flops 1022623744 | bytes 13205888 | tf_op jit(solution)/shard_map/while/body/eval_jaxpr/erp,eipk->eirk/dot_general | solution.py:80
  289.3 6.9 %fusion.179 = f32[6,2,128,256]{3,2,0,1:T(8,128)} fusion(f32[6,2,128,256]{3,2,0,1:T(8,128)} %get-tuple-element.279, s32[]{:T(128)} %get-tuple-element.278, s32[32]{0:T(128)S(1)} %get-tuple-element.260, s32[256,320]{0,1:T(8,128)S(1)} %iota_subtract_fusion.4, bf16[32]{0:T(256)(128)(2,1)S(1)} %get-tuple-element.263, ...), kind=kOutput, calls=%fused_computation.47.clone.3 | convolution fusion | flops 1373634560 | bytes 5833600 | tf_op jit(solution)/shard_map/while/body/eval_jaxpr/eirk,eck->irc/dot_general | solution.py:83
  299.3 7.6 %fusion.178 = bf16[32,2,128,320]{2,3,0,1:T(8,128)(2,1)S(1)} fusion(bf16[32,2,192,320]{3,2,1,0:T(8,128)(2,1)} %get-tuple-element.288, s32[32]{0:T(128)S(1)} %get-tuple-element.267, s32[128,192]{1,0:T(8,128)S(1)} %iota_subtract_fusion.5, bf16[32]{0:T(256)(128)(2,1)S(1)} %get-tuple-element.268, ...), kind=kOutput, calls=%fused_computation.19.clone.clone.clone.clone.clone.2.clone.1 | convolution fusion | flops 1022623744 | bytes 13205888 | tf_op jit(solution)/shard_map/while/body/eval_jaxpr/erp,eipk->eirk/dot_general | solution.py:80
  306.9 6.9 %fusion.179 = f32[6,2,128,256]{3,2,0,1:T(8,128)} fusion(f32[6,2,128,256]{3,2,0,1:T(8,128)} %get-tuple-element.279, s32[]{:T(128)} %get-tuple-element.278, s32[32]{0:T(128)S(1)} %get-tuple-element.260, s32[256,320]{0,1:T(8,128)S(1)} %iota_subtract_fusion.4, bf16[32]{0:T(256)(128)(2,1)S(1)} %get-tuple-element.263, ...), kind=kOutput, calls=%fused_computation.47.clone.3 | convolution fusion | flops 1373634560 | bytes 5833600 | tf_op jit(solution)/shard_map/while/body/eval_jaxpr/eirk,eck->irc/dot_general | solution.py:83
  316.8 7.6 %fusion.178 = bf16[32,2,128,320]{2,3,0,1:T(8,128)(2,1)S(1)} fusion(bf16[32,2,192,320]{3,2,1,0:T(8,128)(2,1)} %get-tuple-element.288, s32[32]{0:T(128)S(1)} %get-tuple-element.267, s32[128,192]{1,0:T(8,128)S(1)} %iota_subtract_fusion.5, bf16[32]{0:T(256)(128)(2,1)S(1)} %get-tuple-element.268, ...), kind=kOutput, calls=%fused_computation.19.clone.clone.clone.clone.clone.2.clone.1 | convolution fusion | flops 1022623744 | bytes 13205888 | tf_op jit(solution)/shard_map/while/body/eval_jaxpr/erp,eipk->eirk/dot_general | solution.py:80
  324.5 6.9 %fusion.179 = f32[6,2,128,256]{3,2,0,1:T(8,128)} fusion(f32[6,2,128,256]{3,2,0,1:T(8,128)} %get-tuple-element.279, s32[]{:T(128)} %get-tuple-element.278, s32[32]{0:T(128)S(1)} %get-tuple-element.260, s32[256,320]{0,1:T(8,128)S(1)} %iota_subtract_fusion.4, bf16[32]{0:T(256)(128)(2,1)S(1)} %get-tuple-element.263, ...), kind=kOutput, calls=%fused_computation.47.clone.3 | convolution fusion | flops 1373634560 | bytes 5833600 | tf_op jit(solution)/shard_map/while/body/eval_jaxpr/eirk,eck->irc/dot_general | solution.py:83
  334.5 7.6 %fusion.178 = bf16[32,2,128,320]{2,3,0,1:T(8,128)(2,1)S(1)} fusion(bf16[32,2,192,320]{3,2,1,0:T(8,128)(2,1)} %get-tuple-element.288, s32[32]{0:T(128)S(1)} %get-tuple-element.267, s32[128,192]{1,0:T(8,128)S(1)} %iota_subtract_fusion.5, bf16[32]{0:T(256)(128)(2,1)S(1)} %get-tuple-element.268, ...), kind=kOutput, calls=%fused_computation.19.clone.clone.clone.clone.clone.2.clone.1 | convolution fusion | flops 1022623744 | bytes 13205888 | tf_op jit(solution)/shard_map/while/body/eval_jaxpr/erp,eipk->eirk/dot_general | solution.py:80
  342.1 6.9 %fusion.179 = f32[6,2,128,256]{3,2,0,1:T(8,128)} fusion(f32[6,2,128,256]{3,2,0,1:T(8,128)} %get-tuple-element.279, s32[]{:T(128)} %get-tuple-element.278, s32[32]{0:T(128)S(1)} %get-tuple-element.260, s32[256,320]{0,1:T(8,128)S(1)} %iota_subtract_fusion.4, bf16[32]{0:T(256)(128)(2,1)S(1)} %get-tuple-element.263, ...), kind=kOutput, calls=%fused_computation.47.clone.3 | convolution fusion | flops 1373634560 | bytes 5833600 | tf_op jit(solution)/shard_map/while/body/eval_jaxpr/eirk,eck->irc/dot_general | solution.py:83
  (75 shorter events, 43.8 us)
Async XLA Ops:
  1.7 8.4 %collective-permute-start = (f32[2,1,4,256]{3,2,1,0:T(4,128)S(1)}, f32[2,1,4,256]{3,2,1,0:T(4,128)S(1)}, u32[]{:S(2)}, u32[]{:S(2)}) collective-permute-start(f32[2,1,4,256]{3,2,1,0:T(4,128)S(1)} %get-tuple-element.184), channel_id=1, source_target_pairs={{0,64},{64,128},{128,192},{1,65},{65,129},{129,193},{2,66},{66,130... | collective-permute-start | bytes 24584 | tf_op jit(solution)/shard_map/ppermute | solution.py:19
  5.2 5.5 %collective-permute-start.1 = (f32[2,1,4,256]{3,2,1,0:T(4,128)S(1)}, f32[2,1,4,256]{3,2,1,0:T(4,128)S(1)}, u32[]{:S(2)}, u32[]{:S(2)}) collective-permute-start(f32[2,1,4,256]{3,2,1,0:T(4,128)S(1)} %get-tuple-element.185), channel_id=1, source_target_pairs={{64,0},{128,64},{192,128},{65,1},{129,65},{193,129},{66,2},{130,66... | collective-permute-start | bytes 24584 | tf_op jit(solution)/shard_map/ppermute | solution.py:21
  11.8 6.4 %collective-permute-start.2 = (f32[2,1,136,4]{3,2,1,0:T(8,128)S(1)}, f32[2,1,136,4]{3,2,1,0:T(8,128)S(1)}, u32[]{:S(2)}, u32[]{:S(2)}) collective-permute-start(f32[2,1,136,4]{3,2,1,0:T(8,128)S(1)} %get-tuple-element.182), channel_id=1, source_target_pairs={{0,32},{1,33},{2,34},{3,35},{4,36},{5,37},{6,38},{7,39},{8,40},{9,... | collective-permute-start | bytes 13064 | tf_op jit(solution)/shard_map/ppermute | solution.py:19
  15.6 6.9 %collective-permute-start.3 = (f32[2,1,136,4]{3,2,1,0:T(8,128)S(1)}, f32[2,1,136,4]{3,2,1,0:T(8,128)S(1)}, u32[]{:S(2)}, u32[]{:S(2)}) collective-permute-start(f32[2,1,136,4]{3,2,1,0:T(8,128)S(1)} %get-tuple-element.183), channel_id=1, source_target_pairs={{32,0},{33,1},{34,2},{35,3},{36,4},{37,5},{38,6},{39,7},{40,8},{41... | collective-permute-start | bytes 13064 | tf_op jit(solution)/shard_map/ppermute | solution.py:21
  154.4 29.9 %copy-start = (bf16[32,1,2,128,256]{4,3,2,1,0:T(8,128)(2,1)}, bf16[32,1,2,128,256]{4,3,2,1,0:T(8,128)(2,1)S(1)}, u32[]{:S(2)}) copy-start(bf16[32,1,2,128,256]{4,3,2,1,0:T(8,128)(2,1)S(1)} %all_to_all.5) | copy-start | bytes 12582916
  154.6 26.8 %collective-permute-start.4 = (bf16[32,2,32,256]{3,2,1,0:T(8,128)(2,1)S(1)}, bf16[32,2,32,256]{3,2,1,0:T(8,128)(2,1)S(1)}, u32[]{:S(2)}, u32[]{:S(2)}) collective-permute-start(bf16[32,2,32,256]{3,2,1,0:T(8,128)(2,1)S(1)} %get-tuple-element.178), channel_id=1, source_target_pairs={{0,64},{64,128},{128,192},{1,65},{65,129},{129,193},{2,66},{66,130... | collective-permute-start | bytes 3145736 | tf_op jit(solution)/shard_map/ppermute | solution.py:19
  157.8 26.5 %collective-permute-start.5 = (bf16[32,2,32,256]{3,2,1,0:T(8,128)(2,1)S(1)}, bf16[32,2,32,256]{3,2,1,0:T(8,128)(2,1)S(1)}, u32[]{:S(2)}, u32[]{:S(2)}) collective-permute-start(bf16[32,2,32,256]{3,2,1,0:T(8,128)(2,1)S(1)} %get-tuple-element.179), channel_id=1, source_target_pairs={{64,0},{128,64},{192,128},{65,1},{129,65},{193,129},{66,2},{130,66... | collective-permute-start | bytes 3145736 | tf_op jit(solution)/shard_map/ppermute | solution.py:21
  181.3 2.9 copy-start.1
  184.3 1.0 copy-start.2
  196.8 23.1 %collective-permute-start.6 = (bf16[32,2,192,32]{2,3,1,0:T(8,128)(2,1)}, bf16[32,2,192,32]{2,3,1,0:T(8,128)(2,1)}, u32[]{:S(2)}, u32[]{:S(2)}) collective-permute-start(bf16[32,2,192,32]{2,3,1,0:T(8,128)(2,1)} %copy.8), channel_id=1, source_target_pairs={{0,32},{1,33},{2,34},{3,35},{4,36},{5,37},{6,38},{7,39},{8,40},{9,... | collective-permute-start | bytes 2359304 | tf_op jit(solution)/shard_map/ppermute | solution.py:19
  202.1 25.9 %collective-permute-start.7 = (bf16[32,2,192,32]{2,3,1,0:T(8,128)(2,1)}, bf16[32,2,192,32]{2,3,1,0:T(8,128)(2,1)}, u32[]{:S(2)}, u32[]{:S(2)}) collective-permute-start(bf16[32,2,192,32]{2,3,1,0:T(8,128)(2,1)} %copy.9), channel_id=1, source_target_pairs={{32,0},{33,1},{34,2},{35,3},{36,4},{37,5},{38,6},{39,7},{40,8},{41... | collective-permute-start | bytes 2359304 | tf_op jit(solution)/shard_map/ppermute | solution.py:21
  231.8 11.6 %copy-start.3 = (s32[32]{0:T(128)S(1)}, s32[32]{0:T(128)}, u32[]{:S(2)}) copy-start(s32[32]{0:T(128)} %param.10) | copy-start | bytes 388
  231.8 11.6 %copy-start.4 = (s32[6,2]{0,1:T(2,128)S(1)}, s32[6,2]{0,1:T(2,128)}, u32[]{:S(2)}) copy-start(s32[6,2]{0,1:T(2,128)} %param.11) | copy-start | bytes 148
